TPU v7x, 32 devices: a whole 2x2x4 slice. The times are simulated.
32 devices in a mesh: view: 4 (over x, core), bx: 4 (over z), by: 2 (over y).
Axes of the slice: x: 2, y: 2, z: 4, core: 2. Of those that a mesh axis runs over, the one named last changes fastest.
Arguments:
- estimate: float32 [256, 32, 128], P('bx', 'by'), may hold values from 0.5 to 2
- observed: float32 [4, 2048, 512], P('view', ('bx', 'by')), may hold values from 0.25 to 4
- destination: int32 [4, 2048, 1], P('view', ('bx', 'by')), may hold values from 0 to 7; in each aligned block of 256 rows (0 to 255, 256 to 511, ..., all dimensions but the last counted through in order) at most 64 rows name the same one
- slot_index: int32 [4, 2048], P('view', ('bx', 'by')), may hold values from 0 to 255
- valid_count: int32 [4, 2048], P('view', ('bx', 'by')), may hold values from 32 to 128
- blend_weight: float32 [4, 2048], P('view', ('bx', 'by')), may hold values from 0.2 to 1
- kernel_x: float32 [4, 17], P('view'), may hold values from 0.1 to 1
- kernel_y: float32 [4, 17], P('view'), may hold values from 0.1 to 1
- kernel_z: float32 [4, 33], P('view'), may hold values from 0.1 to 1
Outputs:
- updated: float32 [256, 32, 128], P('bx', 'by')
Inputs may be any that keep to these rules, and one draw needn't show every extreme that they name: `destination`: in each view, the 256 rows of one device name no brick more than 64 times, a bound that some block reaches.
All inputs are finite; a program needn't handle non-finite values.
Results may differ from a plain program's by a relative error of at most 0.0001.
Values sent between devices are 32-bit elements; how exact they have to be, the bound alone decides.
No kernel may reach another device: no remote copies, remote signals or barrier semaphores. Data moves between devices by JAX's collectives and lax.ppermute only.
A program may use at most 64 MiB of HBM per device.

v0:
```python
import jax
import jax.numpy as jnp
from jax import lax
from jax.sharding import PartitionSpec as P

R = 8
RZ = 16
YP = 4
PV = 512
SLOTS = 256
PIECES = 256


PRIOR_WEIGHT = 0.5


def with_halo(block, sides, width):
    for axis, dim in sides:
        count = lax.axis_size(axis)
        forward = [(i, i + 1) for i in range(count - 1)]
        backward = [(target, source) for source, target in forward]
        low = lax.ppermute(
            lax.slice_in_dim(block, block.shape[dim] - width, None, axis=dim), axis, forward
        )
        high = lax.ppermute(lax.slice_in_dim(block, 0, width, axis=dim), axis, backward)
        block = jnp.concatenate([low, block, high], axis=dim)
    return block


def band_matrix(kernel, extent, radius):
    spread = jnp.arange(extent + 2 * radius)[None, :] - jnp.arange(extent)[:, None]
    offsets = jnp.arange(2 * radius + 1)
    hits = (spread[:, :, None] == offsets[None, None, :]).astype(jnp.float32)
    return jnp.sum(kernel[None, None, :] * hits, axis=2)


def separable(padded, kernel_a, kernel_b, kernel_c):
    rows_x = padded.shape[0] - 2 * R
    rows_y = padded.shape[1] - 2 * R
    depth_cells = padded.shape[2]
    along_first = jnp.einsum(
        "xe,eyz->xyz", band_matrix(kernel_a, rows_x, R), padded, precision=lax.Precision.HIGHEST
    )
    second = jnp.einsum(
        "ye,xez->xyz",
        band_matrix(kernel_b, rows_y, R),
        along_first,
        precision=lax.Precision.HIGHEST,
    )
    depth_band = band_matrix(kernel_c, depth_cells, RZ)[:, RZ : RZ + depth_cells]
    return jnp.einsum("zw,xyw->xyz", depth_band, second, precision=lax.Precision.HIGHEST)


def local(
    estimate,
    observed,
    destination,
    slot_index,
    valid_count,
    blend_weight,
    kernel_x,
    kernel_y,
    kernel_z,
):
    rows_x, rows_y, depth_cells = estimate.shape
    norm_x = kernel_x[0] / jnp.sum(kernel_x[0])
    norm_y = kernel_y[0] / jnp.sum(kernel_y[0])
    norm_z = kernel_z[0] / jnp.sum(kernel_z[0])
    padded = with_halo(estimate, (("bx", 0), ("by", 1)), R)
    blurred = separable(padded, norm_x, norm_y, norm_z)
    count_bx = lax.axis_size("bx")
    count_by = lax.axis_size("by")
    bricks = count_bx * count_by
    capacity = max(4, 2 * PIECES // bricks)
    target = destination[0, :, 0]
    member = (target[:, None] == jnp.arange(bricks)[None, :]).astype(jnp.int32)
    slot_rank = jnp.sum((jnp.cumsum(member, axis=0) - 1) * member, axis=1)
    send_place = target * capacity + slot_rank
    send_rows = jnp.zeros((bricks * capacity, PV), jnp.float32).at[send_place].set(observed[0])
    send_meta = (
        jnp.zeros((bricks * capacity, 2), jnp.int32)
        .at[send_place]
        .set(jnp.stack([slot_index[0], valid_count[0]], axis=1))
    )
    send_weight = jnp.zeros((bricks * capacity,), jnp.float32).at[send_place].set(blend_weight[0])
    recv_rows, recv_meta, recv_weight = (
        lax.all_to_all(
            send_rows.reshape(bricks, capacity, PV),
            ("bx", "by"),
            split_axis=0,
            concat_axis=0,
            tiled=True,
        ),
        lax.all_to_all(
            send_meta.reshape(bricks, capacity, 2),
            ("bx", "by"),
            split_axis=0,
            concat_axis=0,
            tiled=True,
        ),
        lax.all_to_all(
            send_weight.reshape(bricks, capacity),
            ("bx", "by"),
            split_axis=0,
            concat_axis=0,
            tiled=True,
        ),
    )
    recv_rows = recv_rows.reshape(bricks * capacity, PV)
    recv_meta = recv_meta.reshape(bricks * capacity, 2)
    recv_weight = recv_weight.reshape(bricks * capacity)
    depth_index = jnp.arange(depth_cells, dtype=jnp.int32)
    keep_mask = (depth_index[None, :] < recv_meta[:, 1:2]).astype(jnp.float32) * recv_weight[
        :, None
    ]
    weighted = (recv_rows.reshape(-1, YP, depth_cells) * keep_mask[:, None, :]).reshape(-1, PV)
    chooser = (jnp.arange(SLOTS)[:, None] == recv_meta[:, 0][None, :]).astype(jnp.float32)
    data_slots = jnp.dot(chooser, weighted, precision=lax.Precision.HIGHEST)
    cover_slots = jnp.dot(chooser, keep_mask, precision=lax.Precision.HIGHEST)
    data_volume = data_slots.reshape(rows_x, rows_y, depth_cells)
    cover_wide = jnp.broadcast_to(
        cover_slots.reshape(rows_x, rows_y // YP, 1, depth_cells),
        (rows_x, rows_y // YP, YP, depth_cells),
    )
    cover_volume = cover_wide.reshape(rows_x, rows_y, depth_cells)
    ratio_field = (data_volume + PRIOR_WEIGHT * blurred) / ((cover_volume + PRIOR_WEIGHT) * blurred)
    padded_ratio = with_halo(ratio_field, (("bx", 0), ("by", 1)), R)
    correction = separable(padded_ratio, norm_x[::-1], norm_y[::-1], norm_z[::-1])
    log_term = jnp.log(correction)
    logsum = lax.psum(log_term, "view")
    return estimate * jnp.exp(logsum)


def solution(mesh):
    placed = (
        P("bx", "by", None),
        P("view", ("bx", "by"), None),
        P("view", ("bx", "by"), None),
        P("view", ("bx", "by")),
        P("view", ("bx", "by")),
        P("view", ("bx", "by")),
        P("view", None),
        P("view", None),
        P("view", None),
    )
    return jax.shard_map(
        local, mesh=mesh, in_specs=placed, out_specs=P("bx", "by", None), check_vma=False
    )
```

profile of v0, /device:TPU:0, one launch (start us, length us, event | category | flops | bytes accessed | tf_op | source)
XLA Modules:
  0.0 148.1 jit_solution(831064255658808431)
XLA Ops:
  9.6 1.6 %scatter_custom_fusion.2 = f32[512]{0:T(512)S(1)} fusion(s32[256]{0:T(256)S(1)} %bitcast.81, f32[256]{0:T(256)} %bitcast.89, f32[]{:T(128)} %constant.22.clone.1), kind=kCustom, calls=%fused_computation.64 | custom fusion | bytes 2560 | tf_op jit(solution)/shard_map/scatter | solution.py:85
  11.8 7.3 %all-to-all-start.2 = ((f32[8,1,64]{2,1,0:T(1,128)}), f32[8,1,64]{2,1,0:T(1,128)S(1)}, u32[]{:S(2)}, u32[]{:S(2)}) async-start(f32[8,1,64]{2,1,0:T(1,128)} %all_to_all.14), calls=%async_computation.2 | async-start | bytes 8192 | tf_op jit(solution)/shard_map/all_to_all | solution.py:101
  20.0 3.9 %collective-permute-start = (f32[8,16,128]{2,0,1:T(8,128)S(1)}, f32[8,16,128]{2,0,1:T(8,128)S(1)}, u32[]{:S(2)}, u32[]{:S(2)}) collective-permute-start(f32[8,16,128]{2,0,1:T(8,128)S(1)} %copy.60), channel_id=1, source_target_pairs={{0,2},{2,4},{4,6},{1,3},{3,5},{5,7},{8,10},{10,12},{12,14},{9,11},... | collective-permute-start | bytes 196616 | tf_op jit(solution)/shard_map/ppermute | solution.py:22
  24.0 1.3 collective-permute-start.1
  25.3 1.3 reduce_sum.92
  27.3 1.3 reduce_sum.97
  29.3 1.3 reduce_sum.99
  31.4 1.3 broadcast_divide_fusion.4
  32.7 1.2 broadcast_divide_fusion.2
  33.9 1.3 broadcast_divide_fusion
  38.9 6.6 %all-to-all-start = ((s32[8,1,128]{2,1,0:T(1,128)}), s32[8,1,128]{2,1,0:T(1,128)S(1)}, u32[]{:S(2)}, u32[]{:S(2)}) async-start(s32[8,1,128]{2,1,0:T(1,128)} %reshape.213), calls=%async_computation | async-start | bytes 8192 | tf_op jit(solution)/shard_map/all_to_all | solution.py:94
  45.6 2.5 %scatter_custom_fusion.1 = f32[512,512]{1,0:T(8,128)} fusion(s32[256]{0:T(256)S(1)} %bitcast.83, f32[1,256,512]{2,1,0:T(8,128)S(1)} %copy-done, f32[]{:T(128)} %constant.22.clone.1), kind=kCustom, calls=%fused_computation.28 | custom fusion | bytes 1572868 | tf_op jit(solution)/shard_map/scatter | solution.py:79
  49.5 2.5 %all-to-all-done = s32[8,1,128]{2,1,0:T(1,128)S(1)} async-done(((s32[8,1,128]{2,1,0:T(1,128)}), s32[8,1,128]{2,1,0:T(1,128)S(1)}, u32[]{:S(2)}, u32[]{:S(2)}) %all-to-all-start) | async-done | bytes 4128 | tf_op jit(solution)/shard_map/all_to_all | solution.py:94
  51.9 3.6 %all-to-all-start.1 = ((f32[8,64,512]{2,1,0:T(8,128)}), f32[8,64,512]{2,1,0:T(8,128)S(1)}, u32[]{:S(2)}, u32[]{:S(2)}) async-start(f32[8,64,512]{2,1,0:T(8,128)} %bitcast.14), calls=%async_computation.1 | async-start | bytes 2097152 | tf_op jit(solution)/shard_map/all_to_all | solution.py:87
  57.1 3.9 %collective-permute-start.2 = (f32[80,8,128]{2,0,1:T(8,128)S(1)}, f32[80,8,128]{2,0,1:T(8,128)S(1)}, u32[]{:S(2)}, u32[]{:S(2)}) collective-permute-start(f32[80,8,128]{2,0,1:T(8,128)S(1)} %get-tuple-element.13), channel_id=1, source_target_pairs={{0,1},{2,3},{4,5},{6,7},{8,9},{10,11},{12,13},{14,15},{16,17},{18,... | collective-permute-start | bytes 983048 | tf_op jit(solution)/shard_map/ppermute | solution.py:22
  61.0 1.3 collective-permute-start.3
  63.1 7.8 %collective-permute-done.2 = f32[80,8,128]{2,0,1:T(8,128)S(1)} collective-permute-done((f32[80,8,128]{2,0,1:T(8,128)S(1)}, f32[80,8,128]{2,0,1:T(8,128)S(1)}, u32[]{:S(2)}, u32[]{:S(2)}) %collective-permute-start.2) | collective-permute-done | bytes 327712 | tf_op jit(solution)/shard_map/ppermute | solution.py:22
  70.8 4.3 %collective-permute-done.3 = f32[80,8,128]{2,0,1:T(8,128)S(1)} collective-permute-done((f32[80,8,128]{2,0,1:T(8,128)S(1)}, f32[80,8,128]{2,0,1:T(8,128)S(1)}, u32[]{:S(2)}, u32[]{:S(2)}) %collective-permute-start.3) | collective-permute-done | bytes 327712 | tf_op jit(solution)/shard_map/ppermute | solution.py:25
  76.2 1.3 convolution_bitcast_fusion.1
  77.5 2.3 %all-to-all-done.1 = f32[8,64,512]{2,1,0:T(8,128)S(1)} async-done(((f32[8,64,512]{2,1,0:T(8,128)}), f32[8,64,512]{2,1,0:T(8,128)S(1)}, u32[]{:S(2)}, u32[]{:S(2)}) %all-to-all-start.1) | async-done | bytes 1048608 | tf_op jit(solution)/shard_map/all_to_all | solution.py:87
  81.5 1.7 %collective-permute-start.4 = (f32[8,16,128]{2,1,0:T(8,128)S(1)}, f32[8,16,128]{2,1,0:T(8,128)S(1)}, u32[]{:S(2)}, u32[]{:S(2)}) collective-permute-start(f32[8,16,128]{2,1,0:T(8,128)S(1)} %get-tuple-element.15), channel_id=1, source_target_pairs={{0,2},{2,4},{4,6},{1,3},{3,5},{5,7},{8,10},{10,12},{12,14},{9,11},... | collective-permute-start | bytes 196616 | tf_op jit(solution)/shard_map/ppermute | solution.py:22
  83.2 1.3 collective-permute-start.5
  85.1 4.3 %collective-permute-done.5 = f32[8,16,128]{2,1,0:T(8,128)S(1)} collective-permute-done((f32[8,16,128]{2,1,0:T(8,128)S(1)}, f32[8,16,128]{2,1,0:T(8,128)S(1)}, u32[]{:S(2)}, u32[]{:S(2)}) %collective-permute-start.5) | collective-permute-done | bytes 65568 | tf_op jit(solution)/shard_map/ppermute | solution.py:25
  89.4 2.7 %collective-permute-start.6 = (f32[80,8,128]{2,1,0:T(8,128)S(1)}, f32[80,8,128]{2,1,0:T(8,128)S(1)}, u32[]{:S(2)}, u32[]{:S(2)}) collective-permute-start(f32[80,8,128]{2,1,0:T(8,128)S(1)} %get-tuple-element.11), channel_id=1, source_target_pairs={{0,1},{2,3},{4,5},{6,7},{8,9},{10,11},{12,13},{14,15},{16,17},{18,... | collective-permute-start | bytes 983048 | tf_op jit(solution)/shard_map/ppermute | solution.py:22
  92.2 1.5 collective-permute-start.7
  93.6 3.5 %collective-permute-done.6 = f32[80,8,128]{2,1,0:T(8,128)S(1)} collective-permute-done((f32[80,8,128]{2,1,0:T(8,128)S(1)}, f32[80,8,128]{2,1,0:T(8,128)S(1)}, u32[]{:S(2)}, u32[]{:S(2)}) %collective-permute-start.6) | collective-permute-done | bytes 327712 | tf_op jit(solution)/shard_map/ppermute | solution.py:22
  97.1 4.1 %collective-permute-done.7 = f32[80,8,128]{2,1,0:T(8,128)S(1)} collective-permute-done((f32[80,8,128]{2,1,0:T(8,128)S(1)}, f32[80,8,128]{2,1,0:T(8,128)S(1)}, u32[]{:S(2)}, u32[]{:S(2)}) %collective-permute-start.7) | collective-permute-done | bytes 327712 | tf_op jit(solution)/shard_map/ppermute | solution.py:25
  101.4 1.8 %fusion.6 = f32[64,32,128]{2,0,1:T(8,128)S(1)} fusion(f32[80,32,128]{2,1,0:T(8,128)S(1)} %pad_maximum_fusion, f32[64,80]{1,0:T(8,128)S(1)} %get-tuple-element.7), kind=kOutput, calls=%fused_computation.13 | convolution fusion | flops 251658240 | bytes 2379776 | tf_op jit(solution)/shard_map/xe,eyz->xyz/dot_general | solution.py:41
  103.1 1.3 convolution_bitcast_fusion
  104.4 1.4 convolution_log_fusion
  105.8 33.5 %all-reduce.2.cloned.1.call-done = f32[64,16,128]{2,1,0:T(8,128)} async-done(((f32[64,16,128]{2,1,0:T(8,128)}), f32[64,16,128]{2,1,0:T(8,128)}) %all-reduce.2.cloned.1.call-update) | async-done | bytes 524304 | tf_op jit(solution)/shard_map/psum | solution.py:130
  139.3 1.9 %exponential_multiply_fusion = f32[64,16,128]{2,1,0:T(8,128)} fusion(f32[64,16,128]{2,1,0:T(8,128)S(1)} %copy-done.1, f32[64,16,128]{2,1,0:T(8,128)} %all-reduce.2.cloned.1.call-done), kind=kLoop, calls=%fused_computation.30 | loop fusion | flops 131072 | bytes 1572864 | tf_op jit(solution)/shard_map/mul | solution.py:131
  (60 shorter events, 17.8 us)
Async XLA Ops:
  6.5 39.1 %copy-start = (f32[1,256,512]{2,1,0:T(8,128)S(1)}, f32[1,256,512]{2,1,0:T(8,128)}, u32[]{:S(2)}) copy-start(f32[1,256,512]{2,1,0:T(8,128)} %param.10) | copy-start | bytes 1572868
  11.8 27.1 %all-to-all-start.2 = ((f32[8,1,64]{2,1,0:T(1,128)}), f32[8,1,64]{2,1,0:T(1,128)S(1)}, u32[]{:S(2)}, u32[]{:S(2)}) async-start(f32[8,1,64]{2,1,0:T(1,128)} %all_to_all.14), calls=%async_computation.2 | async-start | bytes 8192 | tf_op jit(solution)/shard_map/all_to_all | solution.py:101
  20.0 36.9 %collective-permute-start = (f32[8,16,128]{2,0,1:T(8,128)S(1)}, f32[8,16,128]{2,0,1:T(8,128)S(1)}, u32[]{:S(2)}, u32[]{:S(2)}) collective-permute-start(f32[8,16,128]{2,0,1:T(8,128)S(1)} %copy.60), channel_id=1, source_target_pairs={{0,2},{2,4},{4,6},{1,3},{3,5},{5,7},{8,10},{10,12},{12,14},{9,11},... | collective-permute-start | bytes 196616 | tf_op jit(solution)/shard_map/ppermute | solution.py:22
  24.0 33.1 %collective-permute-start.1 = (f32[8,16,128]{2,0,1:T(8,128)S(1)}, f32[8,16,128]{2,0,1:T(8,128)S(1)}, u32[]{:S(2)}, u32[]{:S(2)}) collective-permute-start(f32[8,16,128]{2,0,1:T(8,128)S(1)} %copy.61), channel_id=1, source_target_pairs={{2,0},{4,2},{6,4},{3,1},{5,3},{7,5},{10,8},{12,10},{14,12},{11,9},... | collective-permute-start | bytes 196616 | tf_op jit(solution)/shard_map/ppermute | solution.py:25
  38.9 13.0 %all-to-all-start = ((s32[8,1,128]{2,1,0:T(1,128)}), s32[8,1,128]{2,1,0:T(1,128)S(1)}, u32[]{:S(2)}, u32[]{:S(2)}) async-start(s32[8,1,128]{2,1,0:T(1,128)} %reshape.213), calls=%async_computation | async-start | bytes 8192 | tf_op jit(solution)/shard_map/all_to_all | solution.py:94
  48.1 8.8 %copy-start.1 = (f32[64,16,128]{2,1,0:T(8,128)S(1)}, f32[64,16,128]{2,1,0:T(8,128)}, u32[]{:S(2)}) copy-start(f32[64,16,128]{2,1,0:T(8,128)} %param.9) | copy-start | bytes 1572868
  51.9 27.9 %all-to-all-start.1 = ((f32[8,64,512]{2,1,0:T(8,128)}), f32[8,64,512]{2,1,0:T(8,128)S(1)}, u32[]{:S(2)}, u32[]{:S(2)}) async-start(f32[8,64,512]{2,1,0:T(8,128)} %bitcast.14), calls=%async_computation.1 | async-start | bytes 2097152 | tf_op jit(solution)/shard_map/all_to_all | solution.py:87
  55.5 83.9 %all-reduce.2.cloned.1.call-start = ((), (), s32[]{:S(2)}) async-start(), calls=%async_computation.3 | async-start | bytes 1048576 | tf_op jit(solution)/shard_map/psum | solution.py:130
  57.1 13.7 %collective-permute-start.2 = (f32[80,8,128]{2,0,1:T(8,128)S(1)}, f32[80,8,128]{2,0,1:T(8,128)S(1)}, u32[]{:S(2)}, u32[]{:S(2)}) collective-permute-start(f32[80,8,128]{2,0,1:T(8,128)S(1)} %get-tuple-element.13), channel_id=1, source_target_pairs={{0,1},{2,3},{4,5},{6,7},{8,9},{10,11},{12,13},{14,15},{16,17},{18,... | collective-permute-start | bytes 983048 | tf_op jit(solution)/shard_map/ppermute | solution.py:22
  61.0 14.1 %collective-permute-start.3 = (f32[80,8,128]{2,0,1:T(8,128)S(1)}, f32[80,8,128]{2,0,1:T(8,128)S(1)}, u32[]{:S(2)}, u32[]{:S(2)}) collective-permute-start(f32[80,8,128]{2,0,1:T(8,128)S(1)} %get-tuple-element.14), channel_id=1, source_target_pairs={{1,0},{3,2},{5,4},{7,6},{9,8},{11,10},{13,12},{15,14},{17,16},{19,... | collective-permute-start | bytes 983048 | tf_op jit(solution)/shard_map/ppermute | solution.py:25
  81.5 3.6 %collective-permute-start.4 = (f32[8,16,128]{2,1,0:T(8,128)S(1)}, f32[8,16,128]{2,1,0:T(8,128)S(1)}, u32[]{:S(2)}, u32[]{:S(2)}) collective-permute-start(f32[8,16,128]{2,1,0:T(8,128)S(1)} %get-tuple-element.15), channel_id=1, source_target_pairs={{0,2},{2,4},{4,6},{1,3},{3,5},{5,7},{8,10},{10,12},{12,14},{9,11},... | collective-permute-start | bytes 196616 | tf_op jit(solution)/shard_map/ppermute | solution.py:22
  83.2 6.2 %collective-permute-start.5 = (f32[8,16,128]{2,1,0:T(8,128)S(1)}, f32[8,16,128]{2,1,0:T(8,128)S(1)}, u32[]{:S(2)}, u32[]{:S(2)}) collective-permute-start(f32[8,16,128]{2,1,0:T(8,128)S(1)} %get-tuple-element.16), channel_id=1, source_target_pairs={{2,0},{4,2},{6,4},{3,1},{5,3},{7,5},{10,8},{12,10},{14,12},{11,9},... | collective-permute-start | bytes 196616 | tf_op jit(solution)/shard_map/ppermute | solution.py:25
  89.4 7.7 %collective-permute-start.6 = (f32[80,8,128]{2,1,0:T(8,128)S(1)}, f32[80,8,128]{2,1,0:T(8,128)S(1)}, u32[]{:S(2)}, u32[]{:S(2)}) collective-permute-start(f32[80,8,128]{2,1,0:T(8,128)S(1)} %get-tuple-element.11), channel_id=1, source_target_pairs={{0,1},{2,3},{4,5},{6,7},{8,9},{10,11},{12,13},{14,15},{16,17},{18,... | collective-permute-start | bytes 983048 | tf_op jit(solution)/shard_map/ppermute | solution.py:22
  92.2 9.1 %collective-permute-start.7 = (f32[80,8,128]{2,1,0:T(8,128)S(1)}, f32[80,8,128]{2,1,0:T(8,128)S(1)}, u32[]{:S(2)}, u32[]{:S(2)}) collective-permute-start(f32[80,8,128]{2,1,0:T(8,128)S(1)} %get-tuple-element.12), channel_id=1, source_target_pairs={{1,0},{3,2},{5,4},{7,6},{9,8},{11,10},{13,12},{15,14},{17,16},{19,... | collective-permute-start | bytes 983048 | tf_op jit(solution)/shard_map/ppermute | solution.py:25
Sparse Core Ops, SparseCore 0:
  105.9 33.3 all-reduce.1
where the time goes:
time: 149 us; the launch traced here: 148 us
  waiting for transfers between devices  62.8 us (42%)
  starting transfers between devices  35.1 us (24%)
  other arithmetic  15.7 us (11%)
  between operations  13.7 us (9%)
  local copies, waits for them, and re-layouts  12.2 us (8%)
  matrix products  8.59 us (6%)
    psum x1, waiting for transfers between devices, local(): logsum = lax.psum(log_term, 'view')  33.5 us
    ppermute x4, waiting for transfers between devices, with_halo(): lax.ppermute(lax.slice_in_dim(block, 0, width, axis=dim), axis, backward)  12.7 us
    ppermute x4, starting transfers between devices, with_halo(): lax.ppermute(lax.slice_in_dim(block, block.shape[dim] - width, None, axis...  12.2 us
    ppermute x4, waiting for transfers between devices, with_halo(): lax.ppermute(lax.slice_in_dim(block, block.shape[dim] - width, None, axis...  11.8 us
    all_to_all x1, starting transfers between devices, local(): lax.all_to_all(send_weight.reshape(bricks, capacity), ('bx', 'by'), split...  7.31 us
    all_to_all x1, starting transfers between devices, local(): lax.all_to_all(send_meta.reshape(bricks, capacity, 2), ('bx', 'by'), spli...  6.62 us
    ppermute x4, starting transfers between devices, with_halo(): lax.ppermute(lax.slice_in_dim(block, 0, width, axis=dim), axis, backward)  5.35 us
    all_to_all x1, starting transfers between devices, local(): lax.all_to_all(send_rows.reshape(bricks, capacity, PV), ('bx', 'by'), spl...  3.56 us
  transfers between devices with their start and end apart: 12, of which 9 were waited for; matrix products, arithmetic and copies ran while one was open for 16% of the time, Pallas kernels for 0%

commit v1 on v0

v1 whole, which is shorter than its diff:
```python
import jax
import jax.numpy as jnp
from jax import lax
from jax.experimental import pallas as pl
from jax.experimental.pallas import tpu as pltpu
from jax.sharding import PartitionSpec as P

R = 8
RZ = 16
YP = 4
PV = 512
SLOTS = 256
PIECES = 256
CX = 64
CY = 16
CZ = 128
PRIOR_WEIGHT = 0.5
F32 = jnp.float32
BF16 = jnp.bfloat16
VM = pl.BlockSpec(memory_space=pltpu.VMEM)
SM = pl.BlockSpec(memory_space=pltpu.SMEM)
GROUP = 64
CHUNK = YP * GROUP + 8


def call(kernel, out_shape, scratch=(), in_specs=None, flops=1 << 22, moved=1 << 20):
    return pl.pallas_call(
        kernel,
        out_shape=[jax.ShapeDtypeStruct(s, F32) for s in out_shape],
        in_specs=in_specs,
        out_specs=[VM] * len(out_shape),
        scratch_shapes=list(scratch),
        compiler_params=pltpu.CompilerParams(vmem_limit_bytes=32 << 20),
        cost_estimate=pl.CostEstimate(flops=flops, bytes_accessed=moved, transcendentals=0),
    )


def three(x):
    high = x.astype(BF16)
    rest = x - high.astype(F32)
    mid = rest.astype(BF16)
    return high, mid, (rest - mid.astype(F32)).astype(BF16)


def two(x):
    high = x.astype(BF16)
    return high, (x - high.astype(F32)).astype(BF16)


def iota(shape, dim):
    return lax.broadcasted_iota(jnp.int32, shape, dim)


def mm(a, b):
    return jnp.dot(a, b, preferred_element_type=F32)


def pack_kernel(observed, target, slot, count, weight, *outs):
    bricks = len(outs)
    me = lax.axis_index("bx") * lax.axis_size("by") + lax.axis_index("by")
    goal = target[...] ^ me
    member = (iota((bricks, PIECES), 0) == goal).astype(F32)
    upto = (iota((PIECES, PIECES), 0) <= iota((PIECES, PIECES), 1)).astype(F32)
    ranks = mm(member.astype(BF16), upto.astype(BF16))
    rank = jnp.sum(member * ranks, axis=0, keepdims=True).astype(jnp.int32) - 1
    place = goal * GROUP + rank
    rows = bricks * GROUP
    pick = (iota((rows, PIECES), 0) == place).astype(F32).astype(BF16)
    keep = jnp.where(iota((CZ, PIECES), 0) < count[...], weight[...], 0.0).T
    weighted = observed[...] * jnp.concatenate([keep] * YP, axis=1)
    packed = sum(mm(pick, part) for part in three(weighted))
    parts = [p.astype(F32) for p in three(weight[...])]
    table = jnp.concatenate(
        [slot[...].astype(F32), count[...].astype(F32)] + parts + [jnp.zeros((3, PIECES), F32)],
        axis=0,
    )
    meta = lax.dot_general(
        table.astype(BF16), pick, (((1,), (1,)), ((), ())), preferred_element_type=F32
    )
    wide = jnp.concatenate(
        [meta[0:2], meta[2:3] + meta[3:4] + meta[4:5], jnp.zeros((5, rows), F32)], axis=0
    )
    lane = iota((8, CZ), 1)
    for s in range(bricks):
        for j in range(YP):
            outs[s][j * GROUP : (j + 1) * GROUP, :] = packed[
                s * GROUP : (s + 1) * GROUP, j * CZ : (j + 1) * CZ
            ]
        pair = wide[:, (s // 2) * CZ : (s // 2 + 1) * CZ]
        if s % 2:
            pair = pltpu.roll(pair, GROUP, 1)
        outs[s][YP * GROUP :, :] = jnp.where(lane < GROUP, pair, 0.0)


def sides():
    odd_x = lax.axis_index("bx") % 2
    odd_y = lax.axis_index("by") % 2
    return odd_x, odd_y


def put_edges(volume, ya, yb, xa, xb):
    odd_x, odd_y = sides()
    ya[...] = volume[pl.ds((1 - odd_y) * (CY - R), R)]
    if yb is not None:
        yb[...] = volume[pl.ds(odd_y * (CY - R), R)]
    xa[...] = volume[:, pl.ds(pl.multiple_of((1 - odd_x) * (CX - R), R), R), :]
    xb[...] = volume[:, pl.ds(pl.multiple_of(odd_x * (CX - R), R), R), :]


def turn_kernel(estimate, turned, ya, *rest):
    for y in range(CY):
        turned[y] = estimate[pl.ds(y, CX, stride=CY), :]
    put_edges(turned, ya, *([None] * (3 - len(rest))), *rest)


def corner_kernel(xa, xb, *outs):
    _, odd_y = sides()
    for phase, out in enumerate(outs):
        start = (odd_y if phase else 1 - odd_y) * (CY - R)
        out[0] = xa[pl.ds(start, R)]
        out[1] = xb[pl.ds(start, R)]


def total(kernel, taps):
    acc = kernel[0, 0]
    for i in range(1, taps):
        acc = acc + kernel[0, i]
    return acc


def spread(own, halos, kx, ky, kz, padded, along_x, along_y, reverse):
    xa, xb, y_sides = halos
    odd_x, odd_y = sides()
    taps, ztaps = 2 * R + 1, 2 * RZ + 1
    xs = [pl.multiple_of((1 - odd_x) * (CX + R), R), pl.multiple_of(odd_x * (CX + R), R)]
    ys = [(1 - odd_y) * (CY + R), odd_y * (CY + R)]
    padded[R : R + CY, R : R + CX, :] = own[...]
    padded[R : R + CY, pl.ds(xs[0], R), :] = xa[...]
    padded[R : R + CY, pl.ds(xs[1], R), :] = xb[...]
    for phase in range(2):
        rows = pl.ds(ys[phase], R)
        if phase < len(y_sides):
            edge, corner = y_sides[phase]
            padded[rows, R : R + CX, :] = edge[...]
            padded[rows, pl.ds(xs[0], R), :] = corner[0]
            padded[rows, pl.ds(xs[1], R), :] = corner[1]
        else:
            padded[rows] = jnp.zeros((R, CX + 2 * R, CZ), F32)

    def tap(kernel, n, i):
        return kernel[0, n - 1 - i] if reverse else kernel[0, i]

    wide = 3 * (CX + 2 * R)
    col, row = iota((CX, wide), 1), iota((CX, wide), 0)
    block = col // (CX + 2 * R)
    gap = col - block * (CX + 2 * R) - row
    band = jnp.zeros((CX, wide), F32)
    for i in range(taps):
        band = jnp.where(gap == i, tap(kx, taps, i), band)
    band = band / total(kx, taps)
    high, low = two(band)
    band_x = jnp.where(block == 1, low.astype(F32), high.astype(F32)).astype(BF16)

    gap = iota((CZ, CZ), 0) - iota((CZ, CZ), 1) + RZ
    band = jnp.zeros((CZ, CZ), F32)
    for i in range(ztaps):
        band = jnp.where(gap == i, tap(kz, ztaps, i), band)
    band = band / total(kz, ztaps) / total(ky, taps)
    high, low = two(band)
    band_z = jnp.concatenate([high, low, high], axis=0)

    for y in range(0, CY + 2 * R, 2):
        stack = []
        for k in range(2):
            high, low = two(padded[y + k])
            stack.append(jnp.concatenate([high, high, low], axis=0))
        both = mm(band_x, jnp.concatenate(stack, axis=1))
        along_x[y] = both[:, :CZ]
        along_x[y + 1] = both[:, CZ:]

    def tile(t, carry):
        at = pl.ds(pl.multiple_of(t * 8, 8), 8)
        acc = [None] * CY
        for i in range(CY + 2 * R):
            value = along_x[i, at, :]
            for y in range(CY):
                if 0 <= i - y < taps:
                    term = tap(ky, taps, i - y) * value
                    acc[y] = term if acc[y] is None else acc[y] + term
        for y in range(CY):
            along_y[y, at, :] = acc[y]
        return carry

    lax.fori_loop(0, CX // 8, tile, 0)
    out = []
    for y in range(0, CY, 4):
        block = along_y[y : y + 4].reshape(4 * CX, CZ)
        high, low = two(block)
        result = mm(jnp.concatenate([high, high, low], axis=1), band_z)
        out += [result[k * CX : (k + 1) * CX] for k in range(4)]
    return out


def split_halos(refs, phases):
    own, xa, xb = refs[:3]
    y_sides = [(refs[3 + 2 * p], refs[4 + 2 * p]) for p in range(phases)]
    return own, (xa, xb, y_sides), refs[3 + 2 * phases :]


def blur_kernel(phases, *refs):
    own, halos, (kx, ky, kz, out, padded, along_x, along_y) = split_halos(refs, phases)
    for y, value in enumerate(spread(own, halos, kx, ky, kz, padded, along_x, along_y, False)):
        out[y] = value


def correct_kernel(phases, *refs):
    own, halos, (kx, ky, kz, mine, other, padded, along_x, along_y) = split_halos(refs, phases)
    values = spread(own, halos, kx, ky, kz, padded, along_x, along_y, True)
    core = lax.axis_index("view") % 2
    half = CY // 2
    for low, high in ((0, 1), (1, 0)):

        @pl.when(core == low)
        def _():
            for y in range(half):
                mine[y] = values[low * half + y]
                other[y] = values[high * half + y]


def ratio_kernel(chunks, *refs):
    parts, blurred = refs[:chunks], refs[chunks]
    ratio, ya, *rest = refs[chunks + 1 :]
    rows = chunks * GROUP
    metas = []
    for c in range(0, chunks, 2):
        odd = pltpu.roll(parts[c + 1][YP * GROUP :, :], GROUP, 1)
        metas.append(parts[c][YP * GROUP :, :] + odd)
    meta = jnp.concatenate(metas, axis=1)
    slot, count, weight = meta[0:1].astype(jnp.int32), meta[1:2].astype(jnp.int32), meta[2:3]
    key = (slot & (YP - 1)) * CX + (slot >> 2)
    chooser = (iota((SLOTS, rows), 0) == key).astype(F32).astype(BF16)
    keep = jnp.where(iota((CZ, rows), 0) < count, weight, 0.0).T

    def gathered(values):
        return sum(mm(chooser, part) for part in three(values))

    cover = gathered(keep)
    for j in range(0, YP, 2):
        values = jnp.concatenate(
            [
                jnp.concatenate([p[k * GROUP : (k + 1) * GROUP, :] for p in parts], axis=0)
                for k in (j, j + 1)
            ],
            axis=1,
        )
        data = gathered(values)
        for q in range(CY // YP):
            at = slice(q * CX, (q + 1) * CX)
            for k in range(2):
                y = YP * q + j + k
                base = blurred[y]
                ratio[y] = (data[at, k * CZ : (k + 1) * CZ] + PRIOR_WEIGHT * base) / (
                    (cover[at] + PRIOR_WEIGHT) * base
                )
    put_edges(ratio, ya, *([None] * (3 - len(rest))), *rest)


def finish_kernel(mine, other, estimate, out):
    core = lax.axis_index("view") % 2
    half = CY // 2
    for low in range(2):

        @pl.when(core == low)
        def _():
            for y in range(CY):
                source = mine if y // half == low else other
                rows = pl.ds(y, CX, stride=CY)
                out[rows, :] = source[y % half] * estimate[rows, :]


def swap(x, axis, mask):
    return lax.ppermute(x, axis, [(i, i ^ mask) for i in range(lax.axis_size(axis))])


def pairs(axis):
    count = lax.axis_size(axis)
    first = [(i, i ^ 1) for i in range(count) if i ^ 1 < count]
    second = [(i, ((i + 1) ^ 1) - 1) for i in range(count)]
    second = [(i, k) for i, k in second if 0 <= k < count]
    return [first] + ([second] if second else [])


def halo(edges, y_phases):
    y_edges, xa, xb = edges[:y_phases], edges[-2], edges[-1]
    x_pairs, y_pairs = pairs("bx"), pairs("by")
    y_got = [lax.ppermute(e, "by", pair) for e, pair in zip(y_edges, y_pairs)]
    xa = lax.ppermute(xa, "bx", x_pairs[0])
    xb = lax.ppermute(xb, "bx", x_pairs[1]) if len(x_pairs) > 1 else jnp.zeros_like(xb)
    corners = call(corner_kernel, [(2, R, R, CZ)] * y_phases, in_specs=[VM] * 2)(xa, xb)
    c_got = [lax.ppermute(c, "by", pair) for c, pair in zip(corners, y_pairs)]
    out = [xa, xb]
    for edge, corner in zip(y_got, c_got):
        out += [edge, corner]
    return out


def generic_exchange(bricks, observed, target, slot, count, weight):
    capacity = max(4, 2 * PIECES // bricks)
    member = (target[:, None] == jnp.arange(bricks)[None, :]).astype(jnp.int32)
    slot_rank = jnp.sum((jnp.cumsum(member, axis=0) - 1) * member, axis=1)
    place = target * capacity + slot_rank
    keep = jnp.where(jnp.arange(CZ)[None, :] < count[:, None], weight[:, None], 0.0)
    weighted = (observed.reshape(-1, YP, CZ) * keep[:, None, :]).reshape(-1, PV)
    facts = jnp.stack([slot.astype(F32), count.astype(F32), weight], axis=1)
    rows = jnp.zeros((bricks * capacity, PV), F32).at[place].set(weighted)
    facts = jnp.zeros((bricks * capacity, 3), F32).at[place].set(facts)

    def exchange(x):
        x = x.reshape(bricks, capacity, -1)
        return lax.all_to_all(x, ("bx", "by"), split_axis=0, concat_axis=0, tiled=True)

    chunks = bricks * capacity // GROUP
    rows = exchange(rows).reshape(chunks, GROUP, YP, CZ).transpose(0, 2, 1, 3)
    facts = exchange(facts).reshape(chunks, GROUP, 3).transpose(0, 2, 1)
    facts = jnp.pad(facts, ((0, 0), (0, 5), (0, CZ - GROUP)))
    both = jnp.concatenate([rows.reshape(chunks, YP * GROUP, CZ), facts], axis=1)
    return [both[c] for c in range(chunks)]


def local(
    estimate,
    observed,
    destination,
    slot_index,
    valid_count,
    blend_weight,
    kernel_x,
    kernel_y,
    kernel_z,
):
    count_bx, count_by = lax.axis_size("bx"), lax.axis_size("by")
    bricks = count_bx * count_by
    y_phases = len(pairs("by"))
    flat = estimate.reshape(CX * CY, CZ)
    edge_shapes = [(R, CX, CZ)] * y_phases + [(CY, R, CZ)] * 2
    brick = (CY, CX, CZ)
    half = (CY // 2, CX, CZ)
    kernels = (kernel_x, kernel_y, kernel_z)
    work = [
        pltpu.VMEM((CY + 2 * R, CX + 2 * R, CZ), F32),
        pltpu.VMEM((CY + 2 * R, CX, CZ), F32),
        pltpu.VMEM(brick, F32),
    ]
    halo_specs = [VM] * (3 + 2 * y_phases) + [SM] * 3

    if bricks * GROUP == 2 * PIECES:
        packed = call(pack_kernel, [(CHUNK, CZ)] * bricks, in_specs=[VM] * 5)(
            observed[0], destination.reshape(1, PIECES), slot_index, valid_count, blend_weight
        )
        chunks = [packed[0]]
        for s in sorted(range(1, bricks), reverse=True):
            pair = [(d, d ^ s) for d in range(bricks)]
            chunks.append(lax.ppermute(packed[s], ("bx", "by"), pair))
    else:
        chunks = generic_exchange(
            bricks,
            observed[0],
            destination[0, :, 0],
            slot_index[0],
            valid_count[0],
            blend_weight[0],
        )

    turned, *edges = call(turn_kernel, [brick] + edge_shapes, in_specs=[VM])(flat)
    around = halo(edges, y_phases)

    def blur(*refs):
        blur_kernel(y_phases, *refs)

    (blurred,) = call(blur, [brick], work, halo_specs)(turned, *around, *kernels)

    def ratios(*refs):
        ratio_kernel(len(chunks), *refs)

    ratio, *edges = call(
        ratios, [brick] + edge_shapes, in_specs=[VM] * (len(chunks) + 1)
    )(*chunks, blurred)
    around = halo(edges, y_phases)

    def correct(*refs):
        correct_kernel(y_phases, *refs)

    mine, other = call(correct, [half, half], work, halo_specs)(ratio, *around, *kernels)
    mine = mine * swap(other, "view", 1)
    mine = mine * swap(mine, "view", 2)
    other = swap(mine, "view", 1)
    (updated,) = call(finish_kernel, [(CX * CY, CZ)], in_specs=[VM] * 3)(mine, other, flat)
    return updated.reshape(CX, CY, CZ)


def solution(mesh):
    placed = (
        P("bx", "by", None),
        P("view", ("bx", "by"), None),
        P("view", ("bx", "by"), None),
        P("view", ("bx", "by")),
        P("view", ("bx", "by")),
        P("view", ("bx", "by")),
        P("view", None),
        P("view", None),
        P("view", None),
    )
    return jax.shard_map(
        local, mesh=mesh, in_specs=placed, out_specs=P("bx", "by", None), check_vma=False
    )
```

time: 149 us -> 65.4 us (0.44)
  the two profiles are of different devices: /device:TPU:0 before, /device:TPU:15 now
where the time goes in v1:
time: 65.4 us; the launch traced here: 65.2 us
  waiting for transfers between devices  28.4 us (43%)
  starting transfers between devices  26.9 us (41%)
  Pallas kernels  7.98 us (12%)
  local copies, waits for them, and re-layouts  1.78 us (3%)
    ppermute x3, waiting for transfers between devices, swap(): lax.ppermute(x, axis, [(i, i ^ mask) for i in range(lax.axis_size(axis))])  9.57 us
    ppermute x3, starting transfers between devices, swap(): lax.ppermute(x, axis, [(i, i ^ mask) for i in range(lax.axis_size(axis))])  8.69 us
    ppermute x2, starting transfers between devices, halo(): lax.ppermute(xb, 'bx', x_pairs[1])  7.1 us
    ppermute x2, waiting for transfers between devices, halo(): lax.ppermute(xb, 'bx', x_pairs[1])  6.6 us
    ppermute x7, starting transfers between devices, local(): chunks.append(lax.ppermute(packed[s], ('bx', 'by'), pair))  5.98 us
    ppermute x2, waiting for transfers between devices, halo(): c_got = [lax.ppermute(c, 'by', pair) for c, pair in zip(corners, y_pairs)]  4.86 us
    ppermute x7, waiting for transfers between devices, local(): chunks.append(lax.ppermute(packed[s], ('bx', 'by'), pair))  4.45 us
    ppermute x2, waiting for transfers between devices, halo(): xa = lax.ppermute(xa, 'bx', x_pairs[0])  2.89 us
  transfers between devices with their start and end apart: 18, of which 11 were waited for; matrix products, arithmetic and copies ran while one was open for 0% of the time, Pallas kernels for 5%

profile of v1, /device:TPU:15, one launch (start us, length us, event | category | flops | bytes accessed | tf_op | source)
XLA Modules:
  0.0 65.2 jit_solution(16835884461477720708)
XLA Ops:
  0.0 1.0 %copy-done = f32[64,16,128]{2,1,0:T(8,128)S(1)} copy-done((f32[64,16,128]{2,1,0:T(8,128)S(1)}, f32[64,16,128]{2,1,0:T(8,128)}, u32[]{:S(2)}) %copy-start) | copy-done | bytes 524312
  1.3 0.3 collective-permute-start.9
  1.6 0.5 copy-done.2
  2.3 0.8 %shard_map.91 = (f32[264,128]{1,0:T(8,128)S(1)}, f32[264,128]{1,0:T(8,128)S(1)}, f32[264,128]{1,0:T(8,128)S(1)}, f32[264,128]{1,0:T(8,128)S(1)}, f32[264,128]{1,...) custom-call(f32[256,512]{1,0:T(8,128)S(1)} %bitcast.6, ...), custom_call_target="tpu_custom_call" | custom-call | flops 4194304 | bytes 1048576 | tf_op jit(solution)/shard_map/pallas_call | solution.py:357
  3.1 2.2 %collective-permute-start = (f32[264,128]{1,0:T(8,128)S(1)}, f32[264,128]{1,0:T(8,128)S(1)}, u32[]{:S(2)}, u32[]{:S(2)}) collective-permute-start(f32[264,128]{1,0:T(8,128)S(1)} %get-tuple-element.24), channel_id=1, source_target_pairs={{0,7},{1,6},{2,5},{3,4},{4,3},{5,2},{6,1},{7,0},{8,15},{9,14},{10,... | collective-permute-start | bytes 405512 | tf_op jit(solution)/shard_map/ppermute | solution.py:363
  5.5 2.0 %collective-permute-start.7 = (f32[16,8,128]{2,1,0:T(8,128)S(1)}, f32[16,8,128]{2,1,0:T(8,128)S(1)}, u32[]{:S(2)}, u32[]{:S(2)}) collective-permute-start(f32[16,8,128]{2,1,0:T(8,128)S(1)} %get-tuple-element.32), channel_id=1, source_target_pairs={{0,2},{2,0},{4,6},{6,4},{1,3},{3,1},{5,7},{7,5},{8,10},{10,8},{12,... | collective-permute-start | bytes 196616 | tf_op jit(solution)/shard_map/ppermute | solution.py:297
  7.5 4.3 %collective-permute-start.8 = (f32[16,8,128]{2,1,0:T(8,128)S(1)}, f32[16,8,128]{2,1,0:T(8,128)S(1)}, u32[]{:S(2)}, u32[]{:S(2)}) collective-permute-start(f32[16,8,128]{2,1,0:T(8,128)S(1)} %get-tuple-element.33), channel_id=1, source_target_pairs={{2,4},{4,2},{3,5},{5,3},{10,12},{12,10},{11,13},{13,11},{18,20},{2... | collective-permute-start | bytes 196616 | tf_op jit(solution)/shard_map/ppermute | solution.py:298
  11.8 2.9 %collective-permute-done.7.xa.refs_1_ = f32[16,8,128]{2,1,0:T(8,128)S(1)} collective-permute-done((f32[16,8,128]{2,1,0:T(8,128)S(1)}, f32[16,8,128]{2,1,0:T(8,128)S(1)}, u32[]{:S(2)}, u32[]{:S(2)}) %collective-permute-start.7) | collective-permute-done | bytes 65568 | tf_op jit(solution)/shard_map/ppermute | solution.py:297
  14.6 4.2 %collective-permute-done.8.xb.refs_2_ = f32[16,8,128]{2,1,0:T(8,128)S(1)} collective-permute-done((f32[16,8,128]{2,1,0:T(8,128)S(1)}, f32[16,8,128]{2,1,0:T(8,128)S(1)}, u32[]{:S(2)}, u32[]{:S(2)}) %collective-permute-start.8) | collective-permute-done | bytes 65568 | tf_op jit(solution)/shard_map/ppermute | solution.py:298
  19.0 0.3 collective-permute-start.2
  19.3 2.7 %collective-permute-done.10.refs_4_ = f32[2,8,8,128]{3,2,1,0:T(8,128)S(1)} collective-permute-done((f32[2,8,8,128]{3,2,1,0:T(8,128)S(1)}, f32[2,8,8,128]{3,2,1,0:T(8,128)S(1)}, u32[]{:S(2)}, u32[]{:S(2)}) %collective-permute-start.10) | collective-permute-done | bytes 65568 | tf_op jit(solution)/shard_map/ppermute | solution.py:300
  21.9 0.4 collective-permute-start.3
  22.4 1.6 %collective-permute-start.4 = (f32[264,128]{1,0:T(8,128)S(1)}, f32[264,128]{1,0:T(8,128)S(1)}, u32[]{:S(2)}, u32[]{:S(2)}) collective-permute-start(f32[264,128]{1,0:T(8,128)S(1)} %get-tuple-element.28), channel_id=1, source_target_pairs={{0,3},{1,2},{2,1},{3,0},{4,7},{5,6},{6,5},{7,4},{8,11},{9,10},{10,... | collective-permute-start | bytes 405512 | tf_op jit(solution)/shard_map/ppermute | solution.py:363
  24.1 1.2 %collective-permute-start.6 = (f32[264,128]{1,0:T(8,128)S(1)}, f32[264,128]{1,0:T(8,128)S(1)}, u32[]{:S(2)}, u32[]{:S(2)}) collective-permute-start(f32[264,128]{1,0:T(8,128)S(1)} %get-tuple-element.30), channel_id=1, source_target_pairs={{0,1},{1,0},{2,3},{3,2},{4,5},{5,4},{6,7},{7,6},{8,9},{9,8},{10,11... | collective-permute-start | bytes 405512 | tf_op jit(solution)/shard_map/ppermute | solution.py:363
  25.3 2.4 %shard_map.94.refs_8_ = f32[16,64,128]{2,1,0:T(8,128)S(1)} custom-call(f32[16,64,128]{2,1,0:T(8,128)S(1)} %get-tuple-element.31.refs_0_, f32[16,8,128]{2,1,0:T(8,128)S(1)} %collective-permute-done.7.xa.refs_1_, f32[16,8,128]{2,1,0:T(8,128)S(1)} %collective-permute-done.8.xb.refs_2_, f32[8,64,128]{2,1,0:T(8,128)S(1)} %collective-permute-done.9.refs_3_, ...), custom_call_target="tpu_custom_call" | custom-call | flops 4194304 | bytes 1048576 | tf_op jit(solution)/shard_map/pallas_call | solution.py:380
  27.7 2.2 %collective-permute-done.3.refs_4_ = f32[264,128]{1,0:T(8,128)S(1)} collective-permute-done((f32[264,128]{1,0:T(8,128)S(1)}, f32[264,128]{1,0:T(8,128)S(1)}, u32[]{:S(2)}, u32[]{:S(2)}) %collective-permute-start.3) | collective-permute-done | bytes 135200 | tf_op jit(solution)/shard_map/ppermute | solution.py:363
  30.2 1.9 %collective-permute-done.5.refs_6_ = f32[264,128]{1,0:T(8,128)S(1)} collective-permute-done((f32[264,128]{1,0:T(8,128)S(1)}, f32[264,128]{1,0:T(8,128)S(1)}, u32[]{:S(2)}, u32[]{:S(2)}) %collective-permute-start.5) | collective-permute-done | bytes 135200 | tf_op jit(solution)/shard_map/ppermute | solution.py:363
  32.1 1.1 %shard_map.95 = (f32[16,64,128]{2,1,0:T(8,128)S(1)}, f32[8,64,128]{2,1,0:T(8,128)S(1)}, f32[16,8,128]{2,1,0:T(8,128)S(1)}, f32[16,8,128]{2,1,0:T(8,128)S(1)}) custom-call(f32[264,128]{1,0:T(8,128)S(1)} %get-tuple-element.23.refs_0_, f32[264,128]{1,0:T(8,128)S(1)} %collective-permute-done.refs_1_, f32[264,128]{1,0:T(8,128)S(1)} %collective-permute-done.1.refs_2_, ...), custom_call_target="tpu_custom_call" | custom-call | flops 4194304 | bytes 1048576 | tf_op jit(solution)/shard_map/pallas_call | solution.py:385
  33.2 1.3 %collective-permute-start.13 = (f32[8,64,128]{2,1,0:T(8,128)S(1)}, f32[8,64,128]{2,1,0:T(8,128)S(1)}, u32[]{:S(2)}, u32[]{:S(2)}) collective-permute-start(f32[8,64,128]{2,1,0:T(8,128)S(1)} %get-tuple-element.38), channel_id=1, source_target_pairs={{0,1},{1,0},{2,3},{3,2},{4,5},{5,4},{6,7},{7,6},{8,9},{9,8},{10,11... | collective-permute-start | bytes 786440 | tf_op jit(solution)/shard_map/ppermute | solution.py:296
  34.5 0.4 collective-permute-start.11
  34.9 2.8 %collective-permute-start.12 = (f32[16,8,128]{2,1,0:T(8,128)S(1)}, f32[16,8,128]{2,1,0:T(8,128)S(1)}, u32[]{:S(2)}, u32[]{:S(2)}) collective-permute-start(f32[16,8,128]{2,1,0:T(8,128)S(1)} %get-tuple-element.37), channel_id=1, source_target_pairs={{2,4},{4,2},{3,5},{5,3},{10,12},{12,10},{11,13},{13,11},{18,20},{2... | collective-permute-start | bytes 196616 | tf_op jit(solution)/shard_map/ppermute | solution.py:298
  37.7 2.4 %collective-permute-done.12.xb.refs_2_ = f32[16,8,128]{2,1,0:T(8,128)S(1)} collective-permute-done((f32[16,8,128]{2,1,0:T(8,128)S(1)}, f32[16,8,128]{2,1,0:T(8,128)S(1)}, u32[]{:S(2)}, u32[]{:S(2)}) %collective-permute-start.12) | collective-permute-done | bytes 65568 | tf_op jit(solution)/shard_map/ppermute | solution.py:298
  40.2 0.9 %collective-permute-start.14 = (f32[2,8,8,128]{3,2,1,0:T(8,128)S(1)}, f32[2,8,8,128]{3,2,1,0:T(8,128)S(1)}, u32[]{:S(2)}, u32[]{:S(2)}) collective-permute-start(f32[2,8,8,128]{3,2,1,0:T(8,128)S(1)} %shard_map.96), channel_id=1, source_target_pairs={{0,1},{1,0},{2,3},{3,2},{4,5},{5,4},{6,7},{7,6},{8,9},{9,8},{10,11... | collective-permute-start | bytes 196616 | tf_op jit(solution)/shard_map/ppermute | solution.py:300
  41.1 2.2 %collective-permute-done.14.refs_4_ = f32[2,8,8,128]{3,2,1,0:T(8,128)S(1)} collective-permute-done((f32[2,8,8,128]{3,2,1,0:T(8,128)S(1)}, f32[2,8,8,128]{3,2,1,0:T(8,128)S(1)}, u32[]{:S(2)}, u32[]{:S(2)}) %collective-permute-start.14) | collective-permute-done | bytes 65568 | tf_op jit(solution)/shard_map/ppermute | solution.py:300
  43.3 2.4 %shard_map.97 = (f32[8,64,128]{2,1,0:T(8,128)S(1)}, f32[8,64,128]{2,1,0:T(8,128)S(1)}) custom-call(f32[16,64,128]{2,1,0:T(8,128)S(1)} %get-tuple-element.35.refs_0_, f32[16,8,128]{2,1,0:T(8,128)S(1)} %collective-permute-done.11.xa.refs_1_, f32[16,8,128]{2,1,0:T(8,128)S(1)} %collective-permute-done.12.xb.refs_2_, ...), custom_call_target="tpu_custom_call" | custom-call | flops 4194304 | bytes 1048576 | tf_op jit(solution)/shard_map/pallas_call | solution.py:393
  45.8 7.1 %collective-permute-start.15 = (f32[8,64,128]{2,1,0:T(8,128)S(1)}, f32[8,64,128]{2,1,0:T(8,128)S(1)}, u32[]{:S(2)}, u32[]{:S(2)}) collective-permute-start(f32[8,64,128]{2,1,0:T(8,128)S(1)} %get-tuple-element.40), channel_id=1, source_target_pairs={{0,8},{8,0},{16,24},{24,16},{1,9},{9,1},{17,25},{25,17},{2,10},{10... | collective-permute-start | bytes 786440 | tf_op jit(solution)/shard_map/ppermute | solution.py:282
  52.8 1.2 %collective-permute-done.15 = f32[8,64,128]{2,1,0:T(8,128)S(1)} collective-permute-done((f32[8,64,128]{2,1,0:T(8,128)S(1)}, f32[8,64,128]{2,1,0:T(8,128)S(1)}, u32[]{:S(2)}, u32[]{:S(2)}) %collective-permute-start.15) | collective-permute-done | bytes 262176 | tf_op jit(solution)/shard_map/ppermute | solution.py:282
  54.1 0.3 collective-permute-start.16
  54.4 7.2 %collective-permute-done.16 = f32[8,64,128]{2,1,0:T(8,128)S(1)} collective-permute-done((f32[8,64,128]{2,1,0:T(8,128)S(1)}, f32[8,64,128]{2,1,0:T(8,128)S(1)}, u32[]{:S(2)}, u32[]{:S(2)}) %collective-permute-start.16) | collective-permute-done | bytes 262176 | tf_op jit(solution)/shard_map/ppermute | solution.py:282
  61.6 1.3 %collective-permute-start.17 = (f32[8,64,128]{2,1,0:T(8,128)S(1)}, f32[8,64,128]{2,1,0:T(8,128)S(1)}, u32[]{:S(2)}, u32[]{:S(2)}) collective-permute-start(f32[8,64,128]{2,1,0:T(8,128)S(1)} %mul.7.mine), channel_id=1, source_target_pairs={{0,8},{8,0},{16,24},{24,16},{1,9},{9,1},{17,25},{25,17},{2,10},{10... | collective-permute-start | bytes 786440 | tf_op jit(solution)/shard_map/ppermute | solution.py:282
  62.9 1.2 %collective-permute-done.17.other = f32[8,64,128]{2,1,0:T(8,128)S(1)} collective-permute-done((f32[8,64,128]{2,1,0:T(8,128)S(1)}, f32[8,64,128]{2,1,0:T(8,128)S(1)}, u32[]{:S(2)}, u32[]{:S(2)}) %collective-permute-start.17) | collective-permute-done | bytes 262176 | tf_op jit(solution)/shard_map/ppermute | solution.py:282
  64.1 1.1 %shard_map.98 = f32[1024,128]{1,0:T(8,128)} custom-call(f32[8,64,128]{2,1,0:T(8,128)S(1)} %mul.7.mine, f32[8,64,128]{2,1,0:T(8,128)S(1)} %collective-permute-done.17.other, f32[1024,128]{1,0:T(8,128)S(1)} %bitcast.5), custom_call_target="tpu_custom_call" | custom-call | flops 4194304 | bytes 1048576 | tf_op jit(solution)/shard_map/pallas_call | solution.py:397
  (34 shorter events, 1.2 us)
Async XLA Ops:
  0.0 1.0 %copy-start = (f32[64,16,128]{2,1,0:T(8,128)S(1)}, f32[64,16,128]{2,1,0:T(8,128)}, u32[]{:S(2)}) copy-start(f32[64,16,128]{2,1,0:T(8,128)} %param.9) | copy-start | bytes 1572868
  1.0 1.0 %copy-start.2 = (f32[1,256,512]{2,1,0:T(8,128)S(1)}, f32[1,256,512]{2,1,0:T(8,128)}, u32[]{:S(2)}) copy-start(f32[1,256,512]{2,1,0:T(8,128)} %param.10) | copy-start | bytes 1572868
  1.0 1.0 %copy-start.7 = (s32[1,256]{1,0:T(1,128)S(1)}, s32[1,256]{1,0:T(1,128)}, u32[]{:S(2)}) copy-start(s32[1,256]{1,0:T(1,128)} %slot.1) | copy-start | bytes 3076
  1.0 1.0 %copy-start.8 = (s32[1,256]{1,0:T(1,128)S(1)}, s32[1,256]{1,0:T(1,128)}, u32[]{:S(2)}) copy-start(s32[1,256]{1,0:T(1,128)} %count.1) | copy-start | bytes 3076
  1.0 1.0 %copy-start.9 = (f32[1,256]{1,0:T(1,128)S(1)}, f32[1,256]{1,0:T(1,128)}, u32[]{:S(2)}) copy-start(f32[1,256]{1,0:T(1,128)} %weight.1) | copy-start | bytes 3076
  1.3 22.8 %collective-permute-start.9 = (f32[8,64,128]{2,1,0:T(8,128)S(1)}, f32[8,64,128]{2,1,0:T(8,128)S(1)}, u32[]{:S(2)}, u32[]{:S(2)}) collective-permute-start(f32[8,64,128]{2,1,0:T(8,128)S(1)} %get-tuple-element.34), channel_id=1, source_target_pairs={{0,1},{1,0},{2,3},{3,2},{4,5},{5,4},{6,7},{7,6},{8,9},{9,8},{10,11... | collective-permute-start | bytes 786440 | tf_op jit(solution)/shard_map/ppermute | solution.py:296
  1.6 0.7 %copy-start.6 = (s32[1,256,1]{1,2,0:T(1,128)S(1)}, s32[1,256,1]{1,2,0:T(1,128)}, u32[]{:S(2)}) copy-start(s32[1,256,1]{1,2,0:T(1,128)} %param.11) | copy-start | bytes 3076
  3.1 19.3 %collective-permute-start = (f32[264,128]{1,0:T(8,128)S(1)}, f32[264,128]{1,0:T(8,128)S(1)}, u32[]{:S(2)}, u32[]{:S(2)}) collective-permute-start(f32[264,128]{1,0:T(8,128)S(1)} %get-tuple-element.24), channel_id=1, source_target_pairs={{0,7},{1,6},{2,5},{3,4},{4,3},{5,2},{6,1},{7,0},{8,15},{9,14},{10,... | collective-permute-start | bytes 405512 | tf_op jit(solution)/shard_map/ppermute | solution.py:363
  5.3 18.7 %collective-permute-start.1 = (f32[264,128]{1,0:T(8,128)S(1)}, f32[264,128]{1,0:T(8,128)S(1)}, u32[]{:S(2)}, u32[]{:S(2)}) collective-permute-start(f32[264,128]{1,0:T(8,128)S(1)} %get-tuple-element.25), channel_id=1, source_target_pairs={{0,6},{1,7},{2,4},{3,5},{4,2},{5,3},{6,0},{7,1},{8,14},{9,15},{10,... | collective-permute-start | bytes 405512 | tf_op jit(solution)/shard_map/ppermute | solution.py:363
  5.5 9.2 %collective-permute-start.7 = (f32[16,8,128]{2,1,0:T(8,128)S(1)}, f32[16,8,128]{2,1,0:T(8,128)S(1)}, u32[]{:S(2)}, u32[]{:S(2)}) collective-permute-start(f32[16,8,128]{2,1,0:T(8,128)S(1)} %get-tuple-element.32), channel_id=1, source_target_pairs={{0,2},{2,0},{4,6},{6,4},{1,3},{3,1},{5,7},{7,5},{8,10},{10,8},{12,... | collective-permute-start | bytes 196616 | tf_op jit(solution)/shard_map/ppermute | solution.py:297
  7.5 11.3 %collective-permute-start.8 = (f32[16,8,128]{2,1,0:T(8,128)S(1)}, f32[16,8,128]{2,1,0:T(8,128)S(1)}, u32[]{:S(2)}, u32[]{:S(2)}) collective-permute-start(f32[16,8,128]{2,1,0:T(8,128)S(1)} %get-tuple-element.33), channel_id=1, source_target_pairs={{2,4},{4,2},{3,5},{5,3},{10,12},{12,10},{11,13},{13,11},{18,20},{2... | collective-permute-start | bytes 196616 | tf_op jit(solution)/shard_map/ppermute | solution.py:298
  18.8 3.1 %collective-permute-start.10 = (f32[2,8,8,128]{3,2,1,0:T(8,128)S(1)}, f32[2,8,8,128]{3,2,1,0:T(8,128)S(1)}, u32[]{:S(2)}, u32[]{:S(2)}) collective-permute-start(f32[2,8,8,128]{3,2,1,0:T(8,128)S(1)} %shard_map.93), channel_id=1, source_target_pairs={{0,1},{1,0},{2,3},{3,2},{4,5},{5,4},{6,7},{7,6},{8,9},{9,8},{10,11... | collective-permute-start | bytes 196616 | tf_op jit(solution)/shard_map/ppermute | solution.py:300
  19.0 8.7 %collective-permute-start.2 = (f32[264,128]{1,0:T(8,128)S(1)}, f32[264,128]{1,0:T(8,128)S(1)}, u32[]{:S(2)}, u32[]{:S(2)}) collective-permute-start(f32[264,128]{1,0:T(8,128)S(1)} %get-tuple-element.26), channel_id=1, source_target_pairs={{0,5},{1,4},{2,7},{3,6},{4,1},{5,0},{6,3},{7,2},{8,13},{9,12},{10,... | collective-permute-start | bytes 405512 | tf_op jit(solution)/shard_map/ppermute | solution.py:363
  21.9 8.0 %collective-permute-start.3 = (f32[264,128]{1,0:T(8,128)S(1)}, f32[264,128]{1,0:T(8,128)S(1)}, u32[]{:S(2)}, u32[]{:S(2)}) collective-permute-start(f32[264,128]{1,0:T(8,128)S(1)} %get-tuple-element.27), channel_id=1, source_target_pairs={{0,4},{1,5},{2,6},{3,7},{4,0},{5,1},{6,2},{7,3},{8,12},{9,13},{10,... | collective-permute-start | bytes 405512 | tf_op jit(solution)/shard_map/ppermute | solution.py:363
  22.4 7.8 %collective-permute-start.4 = (f32[264,128]{1,0:T(8,128)S(1)}, f32[264,128]{1,0:T(8,128)S(1)}, u32[]{:S(2)}, u32[]{:S(2)}) collective-permute-start(f32[264,128]{1,0:T(8,128)S(1)} %get-tuple-element.28), channel_id=1, source_target_pairs={{0,3},{1,2},{2,1},{3,0},{4,7},{5,6},{6,5},{7,4},{8,11},{9,10},{10,... | collective-permute-start | bytes 405512 | tf_op jit(solution)/shard_map/ppermute | solution.py:363
  24.0 8.1 %collective-permute-start.5 = (f32[264,128]{1,0:T(8,128)S(1)}, f32[264,128]{1,0:T(8,128)S(1)}, u32[]{:S(2)}, u32[]{:S(2)}) collective-permute-start(f32[264,128]{1,0:T(8,128)S(1)} %get-tuple-element.29), channel_id=1, source_target_pairs={{0,2},{1,3},{2,0},{3,1},{4,6},{5,7},{6,4},{7,5},{8,10},{9,11},{10,... | collective-permute-start | bytes 405512 | tf_op jit(solution)/shard_map/ppermute | solution.py:363
  24.0 1.2 %copy-start.3 = (f32[1,17]{1,0:T(1,128)S(1)}, f32[1,17]{1,0:T(1,128)}, u32[]{:S(2)}) copy-start(f32[1,17]{1,0:T(1,128)} %refs_5_.3) | copy-start | bytes 208
  24.0 1.2 %copy-start.4 = (f32[1,17]{1,0:T(1,128)S(1)}, f32[1,17]{1,0:T(1,128)}, u32[]{:S(2)}) copy-start(f32[1,17]{1,0:T(1,128)} %refs_6_.3) | copy-start | bytes 208
  24.0 1.2 %copy-start.5 = (f32[1,33]{1,0:T(1,128)S(1)}, f32[1,33]{1,0:T(1,128)}, u32[]{:S(2)}) copy-start(f32[1,33]{1,0:T(1,128)} %refs_7_.3) | copy-start | bytes 400
  24.1 8.1 %collective-permute-start.6 = (f32[264,128]{1,0:T(8,128)S(1)}, f32[264,128]{1,0:T(8,128)S(1)}, u32[]{:S(2)}, u32[]{:S(2)}) collective-permute-start(f32[264,128]{1,0:T(8,128)S(1)} %get-tuple-element.30), channel_id=1, source_target_pairs={{0,1},{1,0},{2,3},{3,2},{4,5},{5,4},{6,7},{7,6},{8,9},{9,8},{10,11... | collective-permute-start | bytes 405512 | tf_op jit(solution)/shard_map/ppermute | solution.py:363
  33.2 10.1 %collective-permute-start.13 = (f32[8,64,128]{2,1,0:T(8,128)S(1)}, f32[8,64,128]{2,1,0:T(8,128)S(1)}, u32[]{:S(2)}, u32[]{:S(2)}) collective-permute-start(f32[8,64,128]{2,1,0:T(8,128)S(1)} %get-tuple-element.38), channel_id=1, source_target_pairs={{0,1},{1,0},{2,3},{3,2},{4,5},{5,4},{6,7},{7,6},{8,9},{9,8},{10,11... | collective-permute-start | bytes 786440 | tf_op jit(solution)/shard_map/ppermute | solution.py:296
  34.5 3.2 %collective-permute-start.11 = (f32[16,8,128]{2,1,0:T(8,128)S(1)}, f32[16,8,128]{2,1,0:T(8,128)S(1)}, u32[]{:S(2)}, u32[]{:S(2)}) collective-permute-start(f32[16,8,128]{2,1,0:T(8,128)S(1)} %get-tuple-element.36), channel_id=1, source_target_pairs={{0,2},{2,0},{4,6},{6,4},{1,3},{3,1},{5,7},{7,5},{8,10},{10,8},{12,... | collective-permute-start | bytes 196616 | tf_op jit(solution)/shard_map/ppermute | solution.py:297
  34.9 5.3 %collective-permute-start.12 = (f32[16,8,128]{2,1,0:T(8,128)S(1)}, f32[16,8,128]{2,1,0:T(8,128)S(1)}, u32[]{:S(2)}, u32[]{:S(2)}) collective-permute-start(f32[16,8,128]{2,1,0:T(8,128)S(1)} %get-tuple-element.37), channel_id=1, source_target_pairs={{2,4},{4,2},{3,5},{5,3},{10,12},{12,10},{11,13},{13,11},{18,20},{2... | collective-permute-start | bytes 196616 | tf_op jit(solution)/shard_map/ppermute | solution.py:298
  40.2 3.2 %collective-permute-start.14 = (f32[2,8,8,128]{3,2,1,0:T(8,128)S(1)}, f32[2,8,8,128]{3,2,1,0:T(8,128)S(1)}, u32[]{:S(2)}, u32[]{:S(2)}) collective-permute-start(f32[2,8,8,128]{3,2,1,0:T(8,128)S(1)} %shard_map.96), channel_id=1, source_target_pairs={{0,1},{1,0},{2,3},{3,2},{4,5},{5,4},{6,7},{7,6},{8,9},{9,8},{10,11... | collective-permute-start | bytes 196616 | tf_op jit(solution)/shard_map/ppermute | solution.py:300
  45.8 8.2 %collective-permute-start.15 = (f32[8,64,128]{2,1,0:T(8,128)S(1)}, f32[8,64,128]{2,1,0:T(8,128)S(1)}, u32[]{:S(2)}, u32[]{:S(2)}) collective-permute-start(f32[8,64,128]{2,1,0:T(8,128)S(1)} %get-tuple-element.40), channel_id=1, source_target_pairs={{0,8},{8,0},{16,24},{24,16},{1,9},{9,1},{17,25},{25,17},{2,10},{10... | collective-permute-start | bytes 786440 | tf_op jit(solution)/shard_map/ppermute | solution.py:282
  54.0 10.1 %copy-start.1 = (f32[64,16,128]{2,1,0:T(8,128)S(1)}, f32[64,16,128]{2,1,0:T(8,128)}, u32[]{:S(2)}) copy-start(f32[64,16,128]{2,1,0:T(8,128)} %param.9) | copy-start | bytes 1572868
  54.1 7.6 %collective-permute-start.16 = (f32[8,64,128]{2,1,0:T(8,128)S(1)}, f32[8,64,128]{2,1,0:T(8,128)S(1)}, u32[]{:S(2)}, u32[]{:S(2)}) collective-permute-start(f32[8,64,128]{2,1,0:T(8,128)S(1)} %mul.6), channel_id=1, source_target_pairs={{0,16},{8,24},{16,0},{24,8},{1,17},{9,25},{17,1},{25,9},{2,18},{10... | collective-permute-start | bytes 786440 | tf_op jit(solution)/shard_map/ppermute | solution.py:282
  61.6 2.5 %collective-permute-start.17 = (f32[8,64,128]{2,1,0:T(8,128)S(1)}, f32[8,64,128]{2,1,0:T(8,128)S(1)}, u32[]{:S(2)}, u32[]{:S(2)}) collective-permute-start(f32[8,64,128]{2,1,0:T(8,128)S(1)} %mul.7.mine), channel_id=1, source_target_pairs={{0,8},{8,0},{16,24},{24,16},{1,9},{9,1},{17,25},{25,17},{2,10},{10... | collective-permute-start | bytes 786440 | tf_op jit(solution)/shard_map/ppermute | solution.py:282
